TPU v7x, 512 devices: a whole 4x4x16 slice. The times are simulated.
512 devices in a mesh: row: 32 (over x, y, core), col: 16 (over z).
Axes of the slice: x: 4, y: 4, z: 16, core: 2. Of those that a mesh axis runs over, the one named last changes fastest.
Arguments:
- features: bfloat16 [65536, 256], P('col', 'row'), may hold values from -6 to 6
- weight: bfloat16 [256, 256], replicated, may hold values from -0.375 to 0.375
- adj_values: bfloat16 [32, 16, 96, 128, 128], P('row', 'col'), may hold values from -0.0625 to 0.0625
- block_rows: int32 [32, 16, 96], P('row', 'col'), may hold values from 0 to 15, as said below
- block_cols: int32 [32, 16, 96], P('row', 'col'), may hold values from 0 to 31
- block_counts: int32 [32, 16], P('row', 'col'), may hold values from 1 to 96, as said below
- cotangent: bfloat16 [65536, 256], P(('row', 'col')), may hold values from -6 to 6
Outputs:
- output: bfloat16 [65536, 256], P(('row', 'col'))
- grad_weight: float32 [256, 256], replicated
- grad_features: bfloat16 [65536, 256], P('col', 'row')
Inputs may be any that keep to these rules, and one draw needn't show every extreme that they name: Within one tile the pairs (block_rows, block_cols) over all 96 slots are distinct. `block_counts`: some tile holds exactly 96 live blocks and some other tile exactly one in every draw.
All inputs are finite; a program needn't handle non-finite values.
Results may differ from a plain program's by a relative error of at most 0.029.
Values may be sent and summed in bfloat16 or wider, within the bound.
A program may use at most 64 MiB of HBM per device.

v0:
```python
import math
import jax
import jax.numpy as jnp
from jax import lax
from jax.sharding import PartitionSpec as P

RB = 16


def block_product(tile_values, tile_rows, tile_cols, live_count, panels, out_blocks, transposed):
    padded = tile_values.shape[0]
    blocks_turn = math.gcd(padded, 16)
    block_size = panels.shape[1]
    columns = panels.shape[2]
    turns_needed = (live_count + blocks_turn - 1) // blocks_turn

    def step(turn_index, running):
        offset = turn_index * blocks_turn
        values_now = lax.dynamic_slice_in_dim(tile_values, offset, blocks_turn, 0)
        row_ids = lax.dynamic_slice_in_dim(tile_rows, offset, blocks_turn, 0)
        col_ids = lax.dynamic_slice_in_dim(tile_cols, offset, blocks_turn, 0)
        is_live = offset + jnp.arange(blocks_turn, dtype=jnp.int32) < live_count
        if transposed:
            picked = jnp.take(panels, row_ids, axis=0)
            product = jnp.einsum(
                "bij,bif->bjf", values_now, picked, preferred_element_type=jnp.float32
            )
            target_ids = col_ids
        else:
            picked = jnp.take(panels, col_ids, axis=0)
            product = jnp.einsum(
                "bij,bjf->bif", values_now, picked, preferred_element_type=jnp.float32
            )
            target_ids = row_ids
        contribution = jnp.where(is_live[:, None, None], product, 0.0)
        return running.at[target_ids].add(contribution)

    start_sum = jnp.zeros((out_blocks, block_size, columns), jnp.float32)
    return lax.fori_loop(0, turns_needed, step, start_sum)


def shards(features, weight, adj_values, block_rows, block_cols, block_counts, cotangent):
    tile_values = adj_values[0, 0]
    tile_rows = block_rows[0, 0]
    tile_cols = block_cols[0, 0]
    live_count = block_counts[0, 0]
    block_size = tile_values.shape[1]
    col_blocks = features.shape[0] // block_size
    node_total = col_blocks * block_size * lax.axis_size("col")
    panel_part = lax.all_gather(features, "row", axis=1, tiled=True)
    panels = panel_part.reshape(col_blocks, block_size, panel_part.shape[1])
    partial_value = block_product(tile_values, tile_rows, tile_cols, live_count, panels, RB, False)
    partial_value = partial_value.reshape(RB * block_size, partial_value.shape[2])
    aggregated = lax.psum_scatter(
        partial_value.astype(jnp.bfloat16), "col", scatter_dimension=0, tiled=True
    )
    preact = jnp.dot(aggregated, weight, preferred_element_type=jnp.float32)
    output = jax.nn.silu(preact).astype(jnp.bfloat16)
    sigmoid_pre = jax.nn.sigmoid(preact)
    slopes = sigmoid_pre * (1.0 + preact * (1.0 - sigmoid_pre))
    deltas = (cotangent.astype(jnp.float32) * slopes).astype(jnp.bfloat16)
    local_grad = jnp.dot(aggregated.T, deltas, preferred_element_type=jnp.float32)
    grad_weight = lax.psum(local_grad, ("row", "col")) * (1.0 / math.sqrt(node_total))
    backward = jnp.dot(deltas, weight.T, preferred_element_type=jnp.float32).astype(jnp.bfloat16)
    back_slab = lax.all_gather(backward, "col", axis=0, tiled=True)
    back_panels = back_slab.reshape(RB, block_size, back_slab.shape[1])
    column_terms = block_product(
        tile_values, tile_rows, tile_cols, live_count, back_panels, col_blocks, True
    )
    column_terms = column_terms.reshape(col_blocks * block_size, column_terms.shape[2])
    grad_features = lax.psum_scatter(
        column_terms.astype(jnp.bfloat16), "row", scatter_dimension=1, tiled=True
    )
    return (output, grad_weight, grad_features)


def solution(mesh):
    return jax.shard_map(
        shards,
        mesh=mesh,
        in_specs=(
            P("col", "row"),
            P(),
            P("row", "col", None, None, None),
            P("row", "col", None),
            P("row", "col", None),
            P("row", "col"),
            P(("row", "col"), None),
        ),
        out_specs=(P(("row", "col"), None), P(), P("col", "row")),
        check_vma=False,
    )
```

profile of v0, /device:TPU:2, one launch (start us, length us, event | category | flops | bytes accessed | tf_op | source)
XLA Modules:
  0.0 847.8 jit_solution(3140927563884392423)
XLA Ops:
  7.2 0.0 all-gather.3.cloned.1.call-start
  7.2 0.7 all-gather.3.cloned.1.call-update
  7.9 0.0 reduce-scatter.3.cloned.1.call-start
  8.6 65.7 %all-gather.3.cloned.1.call-done = bf16[4096,256]{0,1:T(8,128)(2,1)} async-done(((bf16[4096,8]{0,1:T(8,128)(2,1)}), bf16[4096,256]{0,1:T(8,128)(2,1)}) %all-gather.3.cloned.1.call-update) | async-done | bytes 2097168 | tf_op jit(solution)/shard_map/all_gather | solution.py:50
  74.3 4.1 copy.11
  78.4 1.5 broadcast_in_dim.58
  80.0 35.9 %while.20 = (s32[]{:T(128)}, f32[16,128,256]{2,1,0:T(8,128)}, s32[]{:T(128)}, s32[96]{0:T(128)S(1)}, s32[]{:T(128)}, /*index=5*/bf16[96,128,128]{2,1,0:T(8,128)(...) while((s32[]{:T(128)}, f32[16,128,256]{2,1,0:T(8,128)}, ...), condition=%wide.region_2.3_spmd, body=%wide.region_0.2_spmd.sunk | while | flops 135791792 | bytes 12063415 | solution.py:39
  80.0 0.7 compare_and_fusion.4
  80.7 2.2 gather_fusion
  82.9 1.5 convolution_select_fusion.4
  84.5 0.1 compare_select_fusion.8
  84.5 4.3 scatter_fusion
  88.9 0.7 compare_and_fusion.4
  89.6 2.2 gather_fusion
  91.8 1.6 convolution_select_fusion.4
  93.4 0.1 compare_select_fusion.8
  93.4 4.4 scatter_fusion
  97.8 0.7 compare_and_fusion.4
  98.5 2.2 gather_fusion
  100.8 1.5 convolution_select_fusion.4
  102.3 0.1 compare_select_fusion.8
  102.4 4.5 scatter_fusion
  106.8 0.7 compare_and_fusion.4
  107.6 2.2 gather_fusion
  109.8 1.6 convolution_select_fusion.4
  111.4 0.1 compare_select_fusion.8
  111.4 4.4 scatter_fusion
  115.9 2.8 convert_element_type.24
  118.7 0.0 all-gather.5.cloned.1.call-start
  118.8 87.5 %reduce-scatter.3.cloned.1.call-done = bf16[128,256]{1,0:T(8,128)(2,1)} async-done(((bf16[2048,256]{1,0:T(8,128)(2,1)}), bf16[128,256]{1,0:T(8,128)(2,1)}) %reduce-scatter.3.cloned.1.call-update) | async-done | bytes 65552 | tf_op jit(solution)/shard_map/reduce_scatter | solution.py:54
  206.3 1.7 multiply_convert_fusion
  208.0 0.8 convolution_convert_fusion
  208.9 0.0 all-reduce.2.cloned.1.call-start
  208.9 2.8 copy.10
  211.7 0.9 fusion.12
  212.7 0.0 reduce-scatter.5.cloned.1.call-start
  212.7 65.3 %all-gather.5.cloned.1.call-done = bf16[2048,256]{1,0:T(8,128)(2,1)} async-done(((bf16[128,256]{1,0:T(8,128)(2,1)}), bf16[2048,256]{1,0:T(8,128)(2,1)}) %all-gather.5.cloned.1.call-update) | async-done | bytes 1048592 | tf_op jit(solution)/shard_map/all_gather | solution.py:65
  278.1 2.4 broadcast_in_dim.59
  280.5 34.6 %while.21 = (s32[]{:T(128)}, f32[32,128,256]{2,1,0:T(8,128)}, s32[]{:T(128)}, s32[96]{0:T(128)S(1)}, s32[]{:T(128)}, /*index=5*/bf16[96,128,128]{1,2,0:T(8,128)(...) while((s32[]{:T(128)}, f32[32,128,256]{2,1,0:T(8,128)}, ...), condition=%wide.region_7.8_spmd, body=%wide.region_5.7_spmd.sunk | while | flops 135791792 | bytes 12063415 | solution.py:39
  280.5 0.7 compare_and_fusion.5
  281.2 1.8 gather_fusion.1
  283.1 1.6 convolution_select_fusion.5
  284.6 0.1 compare_select_fusion.9
  284.7 4.3 scatter_fusion.1
  289.1 0.7 compare_and_fusion.5
  289.8 1.8 gather_fusion.1
  291.6 1.5 convolution_select_fusion.5
  293.2 0.1 compare_select_fusion.9
  293.3 4.5 scatter_fusion.1
  297.7 0.7 compare_and_fusion.5
  298.5 1.8 gather_fusion.1
  300.3 1.6 convolution_select_fusion.5
  301.9 0.1 compare_select_fusion.9
  301.9 4.5 scatter_fusion.1
  306.4 0.7 compare_and_fusion.5
  307.1 1.8 gather_fusion.1
  309.0 1.6 convolution_select_fusion.5
  310.5 0.1 compare_select_fusion.9
  310.6 4.4 scatter_fusion.1
  315.1 2.5 convert_element_type.30
  317.6 2.9 copy.15
  320.5 418.5 %all-reduce.2.cloned.1.call-done = f32[256,256]{1,0:T(8,128)} async-done(((f32[256,256]{1,0:T(8,128)}), f32[256,256]{1,0:T(8,128)}) %all-reduce.2.cloned.1.call-update) | async-done | bytes 262160 | tf_op jit(solution)/shard_map/psum | solution.py:63
  739.0 1.7 broadcast_multiply_fusion
  740.6 100.6 %reduce-scatter.5.cloned.1.call-done = bf16[4096,8]{0,1:T(8,128)(2,1)} async-done(((bf16[4096,256]{0,1:T(8,128)(2,1)}), bf16[4096,8]{0,1:T(8,128)(2,1)}) %reduce-scatter.5.cloned.1.call-update) | async-done | bytes 65552 | tf_op jit(solution)/shard_map/reduce_scatter | solution.py:71
  (24 shorter events, 0.1 us)
Async XLA Ops:
  7.2 199.1 %copy-start = (bf16[256,256]{1,0:T(8,128)(2,1)S(1)}, bf16[256,256]{1,0:T(8,128)(2,1)}, u32[]{:S(2)}) copy-start(bf16[256,256]{1,0:T(8,128)(2,1)} %param.12) | copy-start | bytes 393220
  7.2 67.2 %all-gather.3.cloned.1.call-start = ((), (), s32[]{:S(2)}) async-start(), calls=%async_computation.2 | async-start | bytes 2162688 | tf_op jit(solution)/shard_map/all_gather | solution.py:50
  7.9 198.4 %reduce-scatter.3.cloned.1.call-start = ((), (), s32[]{:S(2)}) async-start(), calls=%async_computation.3 | async-start | bytes 1114112 | tf_op jit(solution)/shard_map/reduce_scatter | solution.py:54
  78.4 1.5 copy-start.3
  78.4 1.5 copy-start.4
  115.9 90.4 %copy-start.5 = (bf16[128,256]{1,0:T(8,128)(2,1)S(1)}, bf16[128,256]{1,0:T(8,128)(2,1)}, u32[]{:S(2)}) copy-start(bf16[128,256]{1,0:T(8,128)(2,1)} %param.17) | copy-start | bytes 196612
  115.9 93.1 %copy-start.1 = (bf16[96,128,128]{2,1,0:T(8,128)(2,1)S(1)}, bf16[96,128,128]{2,1,0:T(8,128)(2,1)}, u32[]{:S(2)}) copy-start(bf16[96,128,128]{2,1,0:T(8,128)(2,1)} %get-tuple-element.328) | copy-start | bytes 9437188
  118.7 159.3 %all-gather.5.cloned.1.call-start = ((), (), s32[]{:S(2)}) async-start(), calls=%async_computation.5 | async-start | bytes 1114112 | tf_op jit(solution)/shard_map/all_gather | solution.py:65
  208.9 2.9 copy-start.2
  208.9 530.1 %all-reduce.2.cloned.1.call-start = ((), (), s32[]{:S(2)}) async-start(), calls=%async_computation.4 | async-start | bytes 524288 | tf_op jit(solution)/shard_map/psum | solution.py:63
  212.7 628.6 %reduce-scatter.5.cloned.1.call-start = ((), (), s32[]{:S(2)}) async-start(), calls=%async_computation.6 | async-start | bytes 2162688 | tf_op jit(solution)/shard_map/reduce_scatter | solution.py:71
Sparse Core Ops, SparseCore 0:
  11.1 63.1 all-gather.2
  118.9 87.4 reduce-scatter.2
  209.2 68.8 all-gather.4
  284.8 454.1 all-reduce.1
  743.8 97.3 reduce-scatter.4
where the time goes:
time: 850 us; the launch traced here: 848 us
  waiting for transfers between devices  738 us (87%)
  other arithmetic  48.7 us (6%)
  local copies, waits for them, and re-layouts  30 us (4%)
  matrix products  15.8 us (2%)
  between operations  14.5 us (2%)
    psum x1, waiting for transfers between devices, shards(): lax.psum(local_grad, ('row', 'col')) * (1.0 / math.sqrt(node_total))  418 us
    reduce_scatter x1, waiting for transfers between devices, shards(): lax.psum_scatter(column_terms.astype(jnp.bfloat16), 'row', scatter_dimens...  101 us
    reduce_scatter x1, waiting for transfers between devices, shards(): lax.psum_scatter(partial_value.astype(jnp.bfloat16), 'col', scatter_dimen...  87.5 us
    all_gather x1, waiting for transfers between devices, shards(): panel_part = lax.all_gather(features, 'row', axis=1, tiled=True)  65.7 us
    all_gather x1, waiting for transfers between devices, shards(): back_slab = lax.all_gather(backward, 'col', axis=0, tiled=True)  65.3 us
    scatter-add x8, other arithmetic, step(): return running.at[target_ids].add(contribution)  35.2 us
  transfers between devices with their start and end apart: 5, of which 5 were waited for; matrix products, arithmetic and copies ran while one was open for 6% of the time, Pallas kernels for 0%

commit v1 on v0

--- a/solution.py
+++ b/solution.py
@@ -5,6 +5,14 @@
 from jax.sharding import PartitionSpec as P
 
 RB = 16
+
+
+def tiled_gather(shard, axis, dim):
+    size = lax.axis_size(axis)
+    repeats = [size if d == dim else 1 for d in range(shard.ndim)]
+    return lax.all_to_all(
+        jnp.tile(shard, repeats), axis, split_axis=dim, concat_axis=dim, tiled=True
+    )
 
 
 def block_product(tile_values, tile_rows, tile_cols, live_count, panels, out_blocks, transposed):
@@ -62,7 +70,7 @@
     local_grad = jnp.dot(aggregated.T, deltas, preferred_element_type=jnp.float32)
     grad_weight = lax.psum(local_grad, ("row", "col")) * (1.0 / math.sqrt(node_total))
     backward = jnp.dot(deltas, weight.T, preferred_element_type=jnp.float32).astype(jnp.bfloat16)
-    back_slab = lax.all_gather(backward, "col", axis=0, tiled=True)
+    back_slab = tiled_gather(backward, "col", 0)
     back_panels = back_slab.reshape(RB, block_size, back_slab.shape[1])
     column_terms = block_product(
         tile_values, tile_rows, tile_cols, live_count, back_panels, col_blocks, True

time: 850 us -> 799 us (0.940)
  waiting for transfers between devices: 738 us -> 679 us
  starting transfers between devices: 0.2 us -> 8.86 us
    all_gather x1 -> x0, waiting for transfers between devices: 65.3 us -> none  [shards(): back_slab = lax.all_gather(backward, 'col', axis=0, tiled=True)]
    all_to_all x0 -> x1, waiting for transfers between devices: none -> 36.9 us  [tiled_gather(): lax.all_to_all(jnp.tile(shard, repeats), axis, split_axis=dim, concat_axi...]
    psum x1, waiting for transfers between devices: 418 us -> 387 us  [shards(): lax.psum(local_grad, ('row', 'col')) * (1.0 / math.sqrt(node_total))]
    all_to_all x0 -> x1, starting transfers between devices: none -> 8.7 us  [tiled_gather(): lax.all_to_all(jnp.tile(shard, repeats), axis, split_axis=dim, concat_axi...]
where the time goes in v1:
time: 799 us; the launch traced here: 797 us
  waiting for transfers between devices  679 us (85%)
  other arithmetic  48.8 us (6%)
  local copies, waits for them, and re-layouts  31.1 us (4%)
  matrix products  15.2 us (2%)
  between operations  14.5 us (2%)
  starting transfers between devices  8.86 us (1%)
    psum x1, waiting for transfers between devices, shards(): lax.psum(local_grad, ('row', 'col')) * (1.0 / math.sqrt(node_total))  387 us
    reduce_scatter x1, waiting for transfers between devices, shards(): lax.psum_scatter(column_terms.astype(jnp.bfloat16), 'row', scatter_dimens...  101 us
    reduce_scatter x1, waiting for transfers between devices, shards(): lax.psum_scatter(partial_value.astype(jnp.bfloat16), 'col', scatter_dimen...  87.7 us
    all_gather x1, waiting for transfers between devices, shards(): panel_part = lax.all_gather(features, 'row', axis=1, tiled=True)  65.7 us
    all_to_all x1, waiting for transfers between devices, tiled_gather(): lax.all_to_all(jnp.tile(shard, repeats), axis, split_axis=dim, concat_axi...  36.9 us
    scatter-add x8, other arithmetic, step(): return running.at[target_ids].add(contribution)  35.4 us
  transfers between devices with their start and end apart: 5, of which 5 were waited for; matrix products, arithmetic and copies ran while one was open for 6% of the time, Pallas kernels for 0%

profile of v1, /device:TPU:2, one launch (start us, length us, event | category | flops | bytes accessed | tf_op | source)
XLA Modules:
  0.0 797.2 jit_solution(10319304800401131378)
XLA Ops:
  7.2 0.7 all-gather.2.cloned.1.call-update
  7.9 0.0 reduce-scatter.3.cloned.1.call-start
  8.6 65.7 %all-gather.2.cloned.1.call-done = bf16[4096,256]{0,1:T(8,128)(2,1)} async-done(((bf16[4096,8]{0,1:T(8,128)(2,1)}), bf16[4096,256]{0,1:T(8,128)(2,1)}) %all-gather.2.cloned.1.call-update) | async-done | bytes 2097168 | tf_op jit(solution)/shard_map/all_gather | solution.py:58
  74.3 4.1 copy.11
  78.4 1.5 broadcast_in_dim.58
  80.0 36.0 %while.20 = (s32[]{:T(128)}, f32[16,128,256]{2,1,0:T(8,128)}, s32[]{:T(128)}, s32[96]{0:T(128)S(1)}, s32[]{:T(128)}, /*index=5*/bf16[96,128,128]{2,1,0:T(8,128)(...) while((s32[]{:T(128)}, f32[16,128,256]{2,1,0:T(8,128)}, ...), condition=%wide.region_2.3_spmd, body=%wide.region_0.2_spmd.sunk | while | flops 135791792 | bytes 12063415 | solution.py:47
  80.0 0.7 compare_and_fusion.4
  80.7 2.2 gather_fusion
  82.9 1.6 convolution_select_fusion.4
  84.5 0.1 compare_select_fusion.8
  84.6 4.3 scatter_fusion
  88.9 0.7 compare_and_fusion.4
  89.6 2.2 gather_fusion
  91.8 1.6 convolution_select_fusion.4
  93.4 0.1 compare_select_fusion.8
  93.5 4.4 scatter_fusion
  97.9 0.7 compare_and_fusion.4
  98.6 2.2 gather_fusion
  100.8 1.5 convolution_select_fusion.4
  102.4 0.1 compare_select_fusion.8
  102.4 4.5 scatter_fusion
  106.9 0.7 compare_and_fusion.4
  107.6 2.2 gather_fusion
  109.8 1.6 convolution_select_fusion.4
  111.4 0.1 compare_select_fusion.8
  111.5 4.5 scatter_fusion
  115.9 2.7 convert_element_type.24
  118.7 87.7 %reduce-scatter.3.cloned.1.call-done = bf16[128,256]{1,0:T(8,128)(2,1)} async-done(((bf16[2048,256]{1,0:T(8,128)(2,1)}), bf16[128,256]{1,0:T(8,128)(2,1)}) %reduce-scatter.3.cloned.1.call-update) | async-done | bytes 65552 | tf_op jit(solution)/shard_map/reduce_scatter | solution.py:62
  206.4 1.7 multiply_convert_fusion
  208.1 0.2 convolution_convert_fusion
  208.3 1.1 tile.2
  209.4 8.7 %all-to-all-start = ((bf16[16,128,256]{2,1,0:T(8,128)(2,1)}), bf16[16,128,256]{2,1,0:T(8,128)(2,1)}, u32[]{:S(2)}, u32[]{:S(2)}) async-start(bf16[16,128,256]{2,1,0:T(8,128)(2,1)} %tile.2), calls=%async_computation.1 | async-start | bytes 2097152 | tf_op jit(solution)/shard_map/all_to_all | solution.py:13
  218.1 0.0 all-reduce.2.cloned.1.call-start
  218.2 2.8 copy.10
  221.0 0.9 fusion.12
  221.9 0.0 reduce-scatter.5.cloned.1.call-start
  222.0 36.9 %all-to-all-done = bf16[16,128,256]{2,1,0:T(8,128)(2,1)} async-done(((bf16[16,128,256]{2,1,0:T(8,128)(2,1)}), bf16[16,128,256]{2,1,0:T(8,128)(2,1)}, u32[]{:S(2)}, u32[]{:S(2)}) %all-to-all-start) | async-done | bytes 1048608 | tf_op jit(solution)/shard_map/all_to_all | solution.py:13
  258.8 2.4 broadcast_in_dim.59
  261.3 34.7 %while.21 = (s32[]{:T(128)}, f32[32,128,256]{2,1,0:T(8,128)}, s32[]{:T(128)}, s32[96]{0:T(128)S(1)}, s32[]{:T(128)}, /*index=5*/bf16[96,128,128]{1,2,0:T(8,128)(...) while((s32[]{:T(128)}, f32[32,128,256]{2,1,0:T(8,128)}, ...), condition=%wide.region_7.8_spmd, body=%wide.region_5.7_spmd.sunk | while | flops 135791792 | bytes 12063415 | solution.py:47
  261.3 0.7 compare_and_fusion.5
  262.0 1.8 gather_fusion.1
  263.9 1.6 convolution_select_fusion.5
  265.4 0.1 compare_select_fusion.9
  265.5 4.3 scatter_fusion.1
  269.9 0.7 compare_and_fusion.5
  270.6 1.8 gather_fusion.1
  272.4 1.5 convolution_select_fusion.5
  274.0 0.1 compare_select_fusion.9
  274.1 4.5 scatter_fusion.1
  278.5 0.7 compare_and_fusion.5
  279.3 1.8 gather_fusion.1
  281.1 1.6 convolution_select_fusion.5
  282.7 0.1 compare_select_fusion.9
  282.8 4.5 scatter_fusion.1
  287.3 0.7 compare_and_fusion.5
  288.0 1.8 gather_fusion.1
  289.9 1.6 convolution_select_fusion.5
  291.4 0.1 compare_select_fusion.9
  291.5 4.5 scatter_fusion.1
  296.0 2.5 convert_element_type.30
  298.5 3.0 copy.15
  301.4 387.0 %all-reduce.2.cloned.1.call-done = f32[256,256]{1,0:T(8,128)} async-done(((f32[256,256]{1,0:T(8,128)}), f32[256,256]{1,0:T(8,128)}) %all-reduce.2.cloned.1.call-update) | async-done | bytes 262160 | tf_op jit(solution)/shard_map/psum | solution.py:71
  688.4 1.7 broadcast_multiply_fusion
  690.1 100.6 %reduce-scatter.5.cloned.1.call-done = bf16[4096,8]{0,1:T(8,128)(2,1)} async-done(((bf16[4096,256]{0,1:T(8,128)(2,1)}), bf16[4096,8]{0,1:T(8,128)(2,1)}) %reduce-scatter.5.cloned.1.call-update) | async-done | bytes 65552 | tf_op jit(solution)/shard_map/reduce_scatter | solution.py:79
  (24 shorter events, 0.2 us)
Async XLA Ops:
  7.2 199.2 %copy-start = (bf16[256,256]{1,0:T(8,128)(2,1)S(1)}, bf16[256,256]{1,0:T(8,128)(2,1)}, u32[]{:S(2)}) copy-start(bf16[256,256]{1,0:T(8,128)(2,1)} %param.12) | copy-start | bytes 393220
  7.2 67.2 %all-gather.2.cloned.1.call-start = ((), (), s32[]{:S(2)}) async-start(), calls=%async_computation.3 | async-start | bytes 2162688 | tf_op jit(solution)/shard_map/all_gather | solution.py:58
  7.9 198.5 %reduce-scatter.3.cloned.1.call-start = ((), (), s32[]{:S(2)}) async-start(), calls=%async_computation.4 | async-start | bytes 1114112 | tf_op jit(solution)/shard_map/reduce_scatter | solution.py:62
  78.4 1.5 copy-start.3
  78.4 1.5 copy-start.4
  115.9 90.5 %copy-start.5 = (bf16[128,256]{1,0:T(8,128)(2,1)S(1)}, bf16[128,256]{1,0:T(8,128)(2,1)}, u32[]{:S(2)}) copy-start(bf16[128,256]{1,0:T(8,128)(2,1)} %param.17) | copy-start | bytes 196612
  118.7 99.5 %copy-start.1 = (bf16[96,128,128]{2,1,0:T(8,128)(2,1)S(1)}, bf16[96,128,128]{2,1,0:T(8,128)(2,1)}, u32[]{:S(2)}) copy-start(bf16[96,128,128]{2,1,0:T(8,128)(2,1)} %get-tuple-element.327) | copy-start | bytes 9437188
  209.4 49.5 %all-to-all-start = ((bf16[16,128,256]{2,1,0:T(8,128)(2,1)}), bf16[16,128,256]{2,1,0:T(8,128)(2,1)}, u32[]{:S(2)}, u32[]{:S(2)}) async-start(bf16[16,128,256]{2,1,0:T(8,128)(2,1)} %tile.2), calls=%async_computation.1 | async-start | bytes 2097152 | tf_op jit(solution)/shard_map/all_to_all | solution.py:13
  218.1 2.9 copy-start.2
  218.1 470.3 %all-reduce.2.cloned.1.call-start = ((), (), s32[]{:S(2)}) async-start(), calls=%async_computation.5 | async-start | bytes 524288 | tf_op jit(solution)/shard_map/psum | solution.py:71
  221.9 568.8 %reduce-scatter.5.cloned.1.call-start = ((), (), s32[]{:S(2)}) async-start(), calls=%async_computation.6 | async-start | bytes 2162688 | tf_op jit(solution)/shard_map/reduce_scatter | solution.py:79
Sparse Core Ops, SparseCore 0:
  11.1 63.1 all-gather.1
  118.8 87.5 reduce-scatter.2
  225.8 462.5 all-reduce.1
  693.3 97.3 reduce-scatter.4
